TPU v7x, 32 devices: a whole 2x2x4 slice. The times are simulated.
32 devices in a mesh: lon: 8 (over z, x), lat: 4 (over y, core).
Axes of the slice: x: 2, y: 2, z: 4, core: 2. Of those that a mesh axis runs over, the one named last changes fastest.
Arguments:
- control_fields: float32 [2, 4, 544, 1536], P(None, None, 'lon', 'lat'), may hold values from -4 to 4
- unexplained_elevation: float32 [544, 1536], P('lon', 'lat'), may hold values from -6 to 6
- diffusivity: float32 [544, 1536], P('lon', 'lat'), may hold values from 0.15 to 0.49
- depth_levels: int32 [544, 1536], P('lon', 'lat'), may hold values from 0 to 4
- fold_partner: int32 [544], replicated, may hold values from 0 to 543, as said below
- prior_sigmas: float32 [2, 4], replicated, may hold values from 0.5 to 2
- haline_thermal_ratio: float32 [544, 1536], P('lon', 'lat'), may hold values from -0.6 to 0.6
- expansion_coefficients: float32 [2, 4], replicated, may hold values from -3 to 3
Outputs:
- state_fields: float32 [2, 4, 544, 1536], P(None, None, 'lon', 'lat')
- sea_height: float32 [544, 1536], P('lon', 'lat')
Inputs may be any that keep to these rules, and one draw needn't show every extreme that they name: `fold_partner`: column i's fold partner lies in the block of 68 columns with block index (8 - (i div 68)) mod (8); within one block the partners are distinct.
All inputs are finite; a program needn't handle non-finite values.
Results may differ from a plain program's by a relative error of at most 0.0003.
Values sent between devices are 32-bit elements; how exact they have to be, the bound alone decides.
A program may use at most 64 MiB of HBM per device.

v0:
```python
import jax
import jax.numpy as jnp
from jax import lax
from jax.sharding import PartitionSpec as P

PASSES = 4


def extended_2(block, sides, width, periodic):
    for axis, dim in sides:
        count = lax.axis_size(axis)
        forward = [(i, i + 1) for i in range(count - 1)]
        if periodic:
            forward.append((count - 1, 0))
        backward = [(target, source) for source, target in forward]
        low = lax.ppermute(
            lax.slice_in_dim(block, block.shape[dim] - width, None, axis=dim), axis, forward
        )
        high = lax.ppermute(lax.slice_in_dim(block, 0, width, axis=dim), axis, backward)
        block = jnp.concatenate([low, block, high], axis=dim)
    return block


def conductances(coefficients, level_values):
    kappa_padded = coefficients[0]
    wet_padded = (level_values < coefficients[1][None]).astype(jnp.float32)
    row_kappa = kappa_padded[:, 1:-1]
    row_wet = wet_padded[:, :, 1:-1]
    along_lon = (row_kappa[:-1] * row_kappa[1:])[None] * row_wet[:, :-1] * row_wet[:, 1:]
    column_kappa = kappa_padded[1:-1]
    column_wet = wet_padded[:, 1:-1]
    along_lat = (
        (column_kappa[:, :-1] * column_kappa[:, 1:])[None]
        * column_wet[:, :, :-1]
        * column_wet[:, :, 1:]
    )
    return (along_lon[:, 1:], along_lon[:, :-1], along_lat[:, :, 1:], along_lat[:, :, :-1])


def diffuse_once(padded, faces, levels_count):
    east_face, west_face, north_face, south_face = faces
    grid = padded.reshape(2, levels_count, padded.shape[1], padded.shape[2])
    centre = grid[:, :, 1:-1, 1:-1]
    result = (
        centre
        + east_face * (grid[:, :, 2:, 1:-1] - centre)
        + west_face * (grid[:, :, :-2, 1:-1] - centre)
        + north_face * (grid[:, :, 1:-1, 2:] - centre)
        + south_face * (grid[:, :, 1:-1, :-2] - centre)
    )
    return result.reshape(2 * levels_count, padded.shape[1] - 2, padded.shape[2] - 2)


def local(
    control_fields,
    unexplained_elevation,
    diffusivity,
    depth_levels,
    fold_partner,
    prior_sigmas,
    haline_thermal_ratio,
    expansion_coefficients,
):
    levels_count = control_fields.shape[1]
    lon_cells = control_fields.shape[2]
    lat_cells = control_fields.shape[3]
    stacked_rows = 2 * levels_count
    lat_devices = lax.axis_size("lat")
    lon_place = lax.axis_index("lon")
    at_top = (lax.axis_index("lat") == lat_devices - 1).astype(jnp.float32)
    depth_float = depth_levels.astype(jnp.float32)
    level_values = jnp.arange(levels_count, dtype=jnp.float32)[:, None, None]
    wet_cells = (level_values < depth_float[None]).astype(jnp.float32)
    masked = (control_fields * wet_cells[None]).reshape(stacked_rows, lon_cells, lat_cells)
    current = jnp.concatenate([masked, diffusivity[None], depth_float[None]], axis=0)
    margin = 1
    own_columns = lon_place * lon_cells + jnp.arange(lon_cells, dtype=jnp.int32)
    own_partners = fold_partner[own_columns]
    faces = None
    for repeat in range(PASSES):
        extended = extended_2(current, (("lon", 1),), 1, True)
        top_rows = extended[:, margin : margin + lon_cells, lat_cells - 1]
        every_top = lax.all_gather(top_rows, "lon", axis=1, tiled=True)
        folded = jnp.take(every_top, own_partners, axis=1)
        folded = jnp.concatenate(
            [jnp.zeros_like(folded[:, :1]), folded, jnp.zeros_like(folded[:, :1])], axis=1
        )
        padded = extended_2(extended, (("lat", 2),), 1, False)
        padded = padded.at[:, :, lat_cells + 1].add(at_top * folded)
        if repeat == 0:
            faces = conductances(padded[stacked_rows:], level_values)
            padded = padded[:stacked_rows]
            extended = extended[:stacked_rows]
        inner = diffuse_once(padded, faces, levels_count)
        current = inner
    assembled_output = current
    assembled_output = assembled_output.reshape(2, levels_count, lon_cells, lat_cells)
    thermal_grid = prior_sigmas[0][:, None, None] * assembled_output[0]
    saltiness_grid = (
        prior_sigmas[1][:, None, None] * assembled_output[1]
        + haline_thermal_ratio[None] * thermal_grid
    )
    ocean_elevation = unexplained_elevation + jnp.sum(
        expansion_coefficients[0][:, None, None] * thermal_grid
        + expansion_coefficients[1][:, None, None] * saltiness_grid,
        axis=0,
    )
    return (jnp.stack([thermal_grid, saltiness_grid]), ocean_elevation)


def solution(mesh):
    return jax.shard_map(
        local,
        mesh=mesh,
        in_specs=(
            P(None, None, "lon", "lat"),
            P("lon", "lat"),
            P("lon", "lat"),
            P("lon", "lat"),
            P(),
            P(),
            P("lon", "lat"),
            P(),
        ),
        out_specs=(P(None, None, "lon", "lat"), P("lon", "lat")),
        check_vma=False,
    )
```

profile of v0, /device:TPU:1, one launch (start us, length us, event | category | flops | bytes accessed | tf_op | source)
XLA Modules:
  0.0 226.4 jit_solution(13621705072636186898)
XLA Ops:
  3.1 2.1 collective-permute-start
  5.2 3.1 %collective-permute-start.1 = (f32[10,1,384]{2,1,0:T(1,128)S(1)}, f32[10,1,384]{2,1,0:T(1,128)S(1)}, u32[]{:S(2)}, u32[]{:S(2)}) collective-permute-start(f32[10,1,384]{2,1,0:T(1,128)S(1)} %get-tuple-element.74), channel_id=1, source_target_pairs={{4,0},{8,4},{12,8},{16,12},{20,16},{24,20},{28,24},{0,28},{5,1},{9... | collective-permute-start | bytes 46088 | tf_op jit(solution)/shard_map/ppermute | solution.py:19
  10.0 24.6 %all-gather = f32[10,544,1]{0,2,1:T(1,128)S(1)} all-gather(f32[10,68,1]{0,2,1:T(1,128)S(1)} %copy.175), channel_id=2, replica_groups=mesh['lon'=8,'lat'=4] {'lon'}, dimensions={1}, use_global_device_ids=true | all-gather | bytes 24480 | tf_op jit(solution)/shard_map/all_gather | solution.py:83
  35.7 9.0 %collective-permute-start.3 = (f32[10,70,1]{1,2,0:T(1,128)S(1)}, f32[10,70,1]{1,2,0:T(1,128)S(1)}, u32[]{:S(2)}, u32[]{:S(2)}) collective-permute-start(f32[10,70,1]{1,2,0:T(1,128)S(1)} %copy.174), channel_id=1, source_target_pairs={{1,0},{2,1},{3,2},{5,4},{6,5},{7,6},{9,8},{10,9},{11,10},{13,12},{... | collective-permute-start | bytes 8408 | tf_op jit(solution)/shard_map/ppermute | solution.py:19
  44.8 3.3 %collective-permute-start.2 = (f32[10,70,1]{2,1,0:T(8,128)S(1)}, f32[10,70,1]{2,1,0:T(8,128)}, u32[]{:S(2)}, u32[]{:S(2)}) collective-permute-start(f32[10,70,1]{2,1,0:T(8,128)S(1)} %get-tuple-element.71), channel_id=1, source_target_pairs={{0,1},{1,2},{2,3},{4,5},{5,6},{6,7},{8,9},{9,10},{10,11},{12,13},{... | collective-permute-start | bytes 8408 | tf_op jit(solution)/shard_map/ppermute | solution.py:16
  48.7 3.9 %collective-permute-done.2 = f32[10,70,1]{2,1,0:T(8,128)} collective-permute-done((f32[10,70,1]{2,1,0:T(8,128)S(1)}, f32[10,70,1]{2,1,0:T(8,128)}, u32[]{:S(2)}, u32[]{:S(2)}) %collective-permute-start.2) | collective-permute-done | bytes 2832 | tf_op jit(solution)/shard_map/ppermute | solution.py:16
  52.5 1.7 pad_maximum_fusion.3
  54.2 3.6 %scatter-add.14 = f32[10,70,386]{2,1,0:T(8,128)S(1)} dynamic-update-slice(f32[10,70,386]{2,1,0:T(8,128)S(1)} %pad_maximum_fusion.3, f32[10,70,1]{2,1,0:T(8,128)S(1)} %copy.148, s32[]{:T(128)} %constant.128.clone.1, s32[]{:T(128)} %constant.128.clone.1, s32[]{:T(128)} %constant.132.clone.1) | dynamic-update-slice | bytes 5604 | tf_op jit(solution)/shard_map/scatter-add | solution.py:89
  63.2 24.8 %all-gather.1 = f32[8,544,1]{0,2,1:T(1,128)S(1)} all-gather(f32[8,68,1]{0,2,1:T(1,128)S(1)} %copy.154), channel_id=3, replica_groups=mesh['lon'=8,'lat'=4] {'lon'}, dimensions={1}, use_global_device_ids=true | all-gather | bytes 19584 | tf_op jit(solution)/shard_map/all_gather | solution.py:83
  89.2 1.7 copy.153
  91.6 11.1 %collective-permute-start.6 = (f32[8,70,1]{1,0,2:T(8,128)S(1)}, f32[8,70,1]{1,0,2:T(8,128)S(1)}, u32[]{:S(2)}, u32[]{:S(2)}) collective-permute-start(f32[8,70,1]{1,0,2:T(8,128)S(1)} %get-tuple-element.67), channel_id=1, source_target_pairs={{0,1},{1,2},{2,3},{4,5},{5,6},{6,7},{8,9},{9,10},{10,11},{12,13},{... | collective-permute-start | bytes 6728 | tf_op jit(solution)/shard_map/ppermute | solution.py:16
  102.8 1.9 collective-permute-start.7
  104.8 2.8 %collective-permute-done.7 = f32[8,70,1]{1,0,2:T(8,128)S(1)} collective-permute-done((f32[8,70,1]{1,0,2:T(8,128)S(1)}, f32[8,70,1]{1,0,2:T(8,128)S(1)}, u32[]{:S(2)}, u32[]{:S(2)}) %collective-permute-start.7) | collective-permute-done | bytes 2272 | tf_op jit(solution)/shard_map/ppermute | solution.py:19
  107.7 3.5 %pad_maximum_fusion = f32[8,70,386]{1,0,2:T(8,128)} fusion(f32[8,70,1]{1,0,2:T(8,128)S(1)} %collective-permute-done.7, f32[8,1,384]{1,0,2:T(8,128)} %copy.153, f32[8,68,384]{1,0,2:T(8,128)S(1)} %copy.152, f32[8,1,384]{1,0,2:T(8,128)S(1)} %copy.151, f32[8,70,1]{1,0,2:T(8,128)S(1)} %collective-permute-done.6), kind=kLoop, calls=%fused_computation.5 | loop fusion | flops 864640 | bytes 1729280 | tf_op jit(solution)/shard_map/concatenate | solution.py:20
  111.8 2.1 copy.156
  116.5 2.8 %collective-permute-start.9 = (f32[8,1,384]{2,0,1:T(8,128)S(1)}, f32[8,1,384]{2,0,1:T(8,128)S(1)}, u32[]{:S(2)}, u32[]{:S(2)}) collective-permute-start(f32[8,1,384]{2,0,1:T(8,128)S(1)} %copy.158), channel_id=1, source_target_pairs={{4,0},{8,4},{12,8},{16,12},{20,16},{24,20},{28,24},{0,28},{5,1},{9... | collective-permute-start | bytes 36872 | tf_op jit(solution)/shard_map/ppermute | solution.py:19
  119.4 1.8 copy.160
  121.7 25.0 %all-gather.2 = f32[8,544,1]{0,2,1:T(1,128)S(1)} all-gather(f32[8,68,1]{0,2,1:T(1,128)S(1)} %copy.162), channel_id=4, replica_groups=mesh['lon'=8,'lat'=4] {'lon'}, dimensions={1}, use_global_device_ids=true | all-gather | bytes 19584 | tf_op jit(solution)/shard_map/all_gather | solution.py:83
  148.0 1.7 copy.161
  150.4 8.4 %collective-permute-start.10 = (f32[8,70,1]{1,0,2:T(8,128)S(1)}, f32[8,70,1]{1,0,2:T(8,128)S(1)}, u32[]{:S(2)}, u32[]{:S(2)}) collective-permute-start(f32[8,70,1]{1,0,2:T(8,128)S(1)} %get-tuple-element.65), channel_id=1, source_target_pairs={{0,1},{1,2},{2,3},{4,5},{5,6},{6,7},{8,9},{9,10},{10,11},{12,13},{... | collective-permute-start | bytes 6728 | tf_op jit(solution)/shard_map/ppermute | solution.py:16
  158.8 1.9 collective-permute-start.11
  160.9 2.8 %collective-permute-done.11 = f32[8,70,1]{1,0,2:T(8,128)S(1)} collective-permute-done((f32[8,70,1]{1,0,2:T(8,128)S(1)}, f32[8,70,1]{1,0,2:T(8,128)S(1)}, u32[]{:S(2)}, u32[]{:S(2)}) %collective-permute-start.11) | collective-permute-done | bytes 2272 | tf_op jit(solution)/shard_map/ppermute | solution.py:19
  163.7 3.5 %pad_maximum_fusion.1 = f32[8,70,386]{1,0,2:T(8,128)} fusion(f32[8,70,1]{1,0,2:T(8,128)S(1)} %collective-permute-done.11, f32[8,1,384]{1,0,2:T(8,128)} %copy.161, f32[8,68,384]{1,0,2:T(8,128)S(1)} %copy.160, f32[8,1,384]{1,0,2:T(8,128)S(1)} %copy.159, f32[8,70,1]{1,0,2:T(8,128)S(1)} %collective-permute-done.10), kind=kLoop, calls=%fused_computation.6 | loop fusion | flops 864640 | bytes 1729280 | tf_op jit(solution)/shard_map/concatenate | solution.py:20
  167.9 2.1 copy.164
  172.8 1.8 copy.168
  175.0 24.9 %all-gather.3 = f32[8,544,1]{0,2,1:T(1,128)S(1)} all-gather(f32[8,68,1]{0,2,1:T(1,128)S(1)} %copy.170), channel_id=5, replica_groups=mesh['lon'=8,'lat'=4] {'lon'}, dimensions={1}, use_global_device_ids=true | all-gather | bytes 19584 | tf_op jit(solution)/shard_map/all_gather | solution.py:83
  201.2 1.7 copy.169
  203.6 8.4 %collective-permute-start.14 = (f32[8,70,1]{1,0,2:T(8,128)S(1)}, f32[8,70,1]{1,0,2:T(8,128)S(1)}, u32[]{:S(2)}, u32[]{:S(2)}) collective-permute-start(f32[8,70,1]{1,0,2:T(8,128)S(1)} %get-tuple-element.63), channel_id=1, source_target_pairs={{0,1},{1,2},{2,3},{4,5},{5,6},{6,7},{8,9},{9,10},{10,11},{12,13},{... | collective-permute-start | bytes 6728 | tf_op jit(solution)/shard_map/ppermute | solution.py:16
  212.0 1.9 collective-permute-start.15
  214.1 2.8 %collective-permute-done.15 = f32[8,70,1]{1,0,2:T(8,128)S(1)} collective-permute-done((f32[8,70,1]{1,0,2:T(8,128)S(1)}, f32[8,70,1]{1,0,2:T(8,128)S(1)}, u32[]{:S(2)}, u32[]{:S(2)}) %collective-permute-start.15) | collective-permute-done | bytes 2272 | tf_op jit(solution)/shard_map/ppermute | solution.py:19
  216.9 3.5 %pad_maximum_fusion.2 = f32[8,70,386]{1,0,2:T(8,128)} fusion(f32[8,70,1]{1,0,2:T(8,128)S(1)} %collective-permute-done.15, f32[8,1,384]{1,0,2:T(8,128)} %copy.169, f32[8,68,384]{1,0,2:T(8,128)S(1)} %copy.168, f32[8,1,384]{1,0,2:T(8,128)S(1)} %copy.167, f32[8,70,1]{1,0,2:T(8,128)S(1)} %collective-permute-done.14), kind=kLoop, calls=%fused_computation.7 | loop fusion | flops 864640 | bytes 1729280 | tf_op jit(solution)/shard_map/concatenate | solution.py:20
  221.1 2.1 copy.172
  (143 shorter events, 28.8 us)
Async XLA Ops:
  0.6 7.7 %copy-start = (s32[544]{0:T(1024)S(1)}, s32[544]{0:T(1024)}, u32[]{:S(2)}) copy-start(s32[544]{0:T(1024)} %param.22) | copy-start | bytes 6532
  3.1 32.2 %collective-permute-start = (f32[10,1,384]{2,1,0:T(1,128)S(1)}, f32[10,1,384]{2,1,0:T(1,128)S(1)}, u32[]{:S(2)}, u32[]{:S(2)}) collective-permute-start(f32[10,1,384]{2,1,0:T(1,128)S(1)} %get-tuple-element.73), channel_id=1, source_target_pairs={{0,4},{4,8},{8,12},{12,16},{16,20},{20,24},{24,28},{28,0},{1,5},{5... | collective-permute-start | bytes 46088 | tf_op jit(solution)/shard_map/ppermute | solution.py:16
  5.2 30.1 %collective-permute-start.1 = (f32[10,1,384]{2,1,0:T(1,128)S(1)}, f32[10,1,384]{2,1,0:T(1,128)S(1)}, u32[]{:S(2)}, u32[]{:S(2)}) collective-permute-start(f32[10,1,384]{2,1,0:T(1,128)S(1)} %get-tuple-element.74), channel_id=1, source_target_pairs={{4,0},{8,4},{12,8},{16,12},{20,16},{24,20},{28,24},{0,28},{5,1},{9... | collective-permute-start | bytes 46088 | tf_op jit(solution)/shard_map/ppermute | solution.py:19
  35.7 12.4 %collective-permute-start.3 = (f32[10,70,1]{1,2,0:T(1,128)S(1)}, f32[10,70,1]{1,2,0:T(1,128)S(1)}, u32[]{:S(2)}, u32[]{:S(2)}) collective-permute-start(f32[10,70,1]{1,2,0:T(1,128)S(1)} %copy.174), channel_id=1, source_target_pairs={{1,0},{2,1},{3,2},{5,4},{6,5},{7,6},{9,8},{10,9},{11,10},{13,12},{... | collective-permute-start | bytes 8408 | tf_op jit(solution)/shard_map/ppermute | solution.py:19
  44.8 7.7 %collective-permute-start.2 = (f32[10,70,1]{2,1,0:T(8,128)S(1)}, f32[10,70,1]{2,1,0:T(8,128)}, u32[]{:S(2)}, u32[]{:S(2)}) collective-permute-start(f32[10,70,1]{2,1,0:T(8,128)S(1)} %get-tuple-element.71), channel_id=1, source_target_pairs={{0,1},{1,2},{2,3},{4,5},{5,6},{6,7},{8,9},{9,10},{10,11},{12,13},{... | collective-permute-start | bytes 8408 | tf_op jit(solution)/shard_map/ppermute | solution.py:16
  60.4 28.8 %collective-permute-start.5 = (f32[8,1,384]{2,0,1:T(8,128)S(1)}, f32[8,1,384]{2,0,1:T(8,128)S(1)}, u32[]{:S(2)}, u32[]{:S(2)}) collective-permute-start(f32[8,1,384]{2,0,1:T(8,128)S(1)} %copy.150), channel_id=1, source_target_pairs={{4,0},{8,4},{12,8},{16,12},{20,16},{24,20},{28,24},{0,28},{5,1},{9... | collective-permute-start | bytes 36872 | tf_op jit(solution)/shard_map/ppermute | solution.py:19
  61.9 26.7 %collective-permute-start.4 = (f32[8,1,384]{2,0,1:T(8,128)S(1)}, f32[8,1,384]{2,0,1:T(8,128)S(1)}, u32[]{:S(2)}, u32[]{:S(2)}) collective-permute-start(f32[8,1,384]{2,0,1:T(8,128)S(1)} %copy.149), channel_id=1, source_target_pairs={{0,4},{4,8},{8,12},{12,16},{16,20},{20,24},{24,28},{28,0},{1,5},{5... | collective-permute-start | bytes 36872 | tf_op jit(solution)/shard_map/ppermute | solution.py:16
  91.6 13.2 %collective-permute-start.6 = (f32[8,70,1]{1,0,2:T(8,128)S(1)}, f32[8,70,1]{1,0,2:T(8,128)S(1)}, u32[]{:S(2)}, u32[]{:S(2)}) collective-permute-start(f32[8,70,1]{1,0,2:T(8,128)S(1)} %get-tuple-element.67), channel_id=1, source_target_pairs={{0,1},{1,2},{2,3},{4,5},{5,6},{6,7},{8,9},{9,10},{10,11},{12,13},{... | collective-permute-start | bytes 6728 | tf_op jit(solution)/shard_map/ppermute | solution.py:16
  102.8 4.9 %collective-permute-start.7 = (f32[8,70,1]{1,0,2:T(8,128)S(1)}, f32[8,70,1]{1,0,2:T(8,128)S(1)}, u32[]{:S(2)}, u32[]{:S(2)}) collective-permute-start(f32[8,70,1]{1,0,2:T(8,128)S(1)} %get-tuple-element.68), channel_id=1, source_target_pairs={{1,0},{2,1},{3,2},{5,4},{6,5},{7,6},{9,8},{10,9},{11,10},{13,12},{... | collective-permute-start | bytes 6728 | tf_op jit(solution)/shard_map/ppermute | solution.py:19
  111.2 2.8 %copy-start.2 = (f32[4,68,384]{2,1,0:T(8,128)S(1)}, f32[4,68,384]{2,1,0:T(8,128)}, u32[]{:S(2)}) copy-start(f32[4,68,384]{2,1,0:T(8,128)} %copy-done.1) | copy-start | bytes 1253380
  111.2 2.8 %copy-start.6 = (f32[4,68,384]{2,1,0:T(8,128)S(1)}, f32[4,68,384]{2,1,0:T(8,128)}, u32[]{:S(2)}) copy-start(f32[4,68,384]{2,1,0:T(8,128)} %copy-done.5) | copy-start | bytes 1253380
  111.2 2.8 %copy-start.10 = (f32[4,68,384]{2,1,0:T(8,128)S(1)}, f32[4,68,384]{2,1,0:T(8,128)}, u32[]{:S(2)}) copy-start(f32[4,68,384]{2,1,0:T(8,128)} %copy-done.9) | copy-start | bytes 1253380
  111.2 2.8 %copy-start.14 = (f32[4,68,384]{2,1,0:T(8,128)S(1)}, f32[4,68,384]{2,1,0:T(8,128)}, u32[]{:S(2)}) copy-start(f32[4,68,384]{2,1,0:T(8,128)} %copy-done.13) | copy-start | bytes 1253380
  115.0 4.3 %copy-start.18 = (f32[2,4,68,384]{3,2,1,0:T(8,128)}, f32[2,4,68,384]{3,2,1,0:T(8,128)S(1)}, u32[]{:S(2)}) copy-start(f32[2,4,68,384]{3,2,1,0:T(8,128)S(1)} %fusion.17) | copy-start | bytes 2506756
  115.0 32.3 %collective-permute-start.8 = (f32[8,1,384]{2,0,1:T(8,128)S(1)}, f32[8,1,384]{2,0,1:T(8,128)S(1)}, u32[]{:S(2)}, u32[]{:S(2)}) collective-permute-start(f32[8,1,384]{2,0,1:T(8,128)S(1)} %copy.157), channel_id=1, source_target_pairs={{0,4},{4,8},{8,12},{12,16},{16,20},{20,24},{24,28},{28,0},{1,5},{5... | collective-permute-start | bytes 36872 | tf_op jit(solution)/shard_map/ppermute | solution.py:16
  116.5 31.4 %collective-permute-start.9 = (f32[8,1,384]{2,0,1:T(8,128)S(1)}, f32[8,1,384]{2,0,1:T(8,128)S(1)}, u32[]{:S(2)}, u32[]{:S(2)}) collective-permute-start(f32[8,1,384]{2,0,1:T(8,128)S(1)} %copy.158), channel_id=1, source_target_pairs={{4,0},{8,4},{12,8},{16,12},{20,16},{24,20},{28,24},{0,28},{5,1},{9... | collective-permute-start | bytes 36872 | tf_op jit(solution)/shard_map/ppermute | solution.py:19
  150.4 10.5 %collective-permute-start.10 = (f32[8,70,1]{1,0,2:T(8,128)S(1)}, f32[8,70,1]{1,0,2:T(8,128)S(1)}, u32[]{:S(2)}, u32[]{:S(2)}) collective-permute-start(f32[8,70,1]{1,0,2:T(8,128)S(1)} %get-tuple-element.65), channel_id=1, source_target_pairs={{0,1},{1,2},{2,3},{4,5},{5,6},{6,7},{8,9},{9,10},{10,11},{12,13},{... | collective-permute-start | bytes 6728 | tf_op jit(solution)/shard_map/ppermute | solution.py:16
  158.8 4.9 %collective-permute-start.11 = (f32[8,70,1]{1,0,2:T(8,128)S(1)}, f32[8,70,1]{1,0,2:T(8,128)S(1)}, u32[]{:S(2)}, u32[]{:S(2)}) collective-permute-start(f32[8,70,1]{1,0,2:T(8,128)S(1)} %get-tuple-element.66), channel_id=1, source_target_pairs={{1,0},{2,1},{3,2},{5,4},{6,5},{7,6},{9,8},{10,9},{11,10},{13,12},{... | collective-permute-start | bytes 6728 | tf_op jit(solution)/shard_map/ppermute | solution.py:19
  167.2 2.8 %copy-start.3 = (f32[4,68,384]{2,1,0:T(8,128)S(1)}, f32[4,68,384]{2,1,0:T(8,128)}, u32[]{:S(2)}) copy-start(f32[4,68,384]{2,1,0:T(8,128)} %copy-done.1) | copy-start | bytes 1253380
  167.2 2.8 %copy-start.7 = (f32[4,68,384]{2,1,0:T(8,128)S(1)}, f32[4,68,384]{2,1,0:T(8,128)}, u32[]{:S(2)}) copy-start(f32[4,68,384]{2,1,0:T(8,128)} %copy-done.5) | copy-start | bytes 1253380
  167.2 2.8 %copy-start.11 = (f32[4,68,384]{2,1,0:T(8,128)S(1)}, f32[4,68,384]{2,1,0:T(8,128)}, u32[]{:S(2)}) copy-start(f32[4,68,384]{2,1,0:T(8,128)} %copy-done.9) | copy-start | bytes 1253380
  167.2 2.8 %copy-start.15 = (f32[4,68,384]{2,1,0:T(8,128)S(1)}, f32[4,68,384]{2,1,0:T(8,128)}, u32[]{:S(2)}) copy-start(f32[4,68,384]{2,1,0:T(8,128)} %copy-done.13) | copy-start | bytes 1253380
  170.0 2.6 %copy-start.22 = (f32[2,4]{1,0:T(2,128)S(1)}, f32[2,4]{1,0:T(2,128)}, u32[]{:S(2)}) copy-start(f32[2,4]{1,0:T(2,128)} %param.25) | copy-start | bytes 100
  170.0 2.6 %copy-start.23 = (f32[2,4]{1,0:T(2,128)S(1)}, f32[2,4]{1,0:T(2,128)}, u32[]{:S(2)}) copy-start(f32[2,4]{1,0:T(2,128)} %param.23) | copy-start | bytes 100
  171.1 30.1 %collective-permute-start.13 = (f32[8,1,384]{2,0,1:T(8,128)S(1)}, f32[8,1,384]{2,0,1:T(8,128)S(1)}, u32[]{:S(2)}, u32[]{:S(2)}) collective-permute-start(f32[8,1,384]{2,0,1:T(8,128)S(1)} %copy.166), channel_id=1, source_target_pairs={{4,0},{8,4},{12,8},{16,12},{20,16},{24,20},{28,24},{0,28},{5,1},{9... | collective-permute-start | bytes 36872 | tf_op jit(solution)/shard_map/ppermute | solution.py:19
  172.6 28.0 %collective-permute-start.12 = (f32[8,1,384]{2,0,1:T(8,128)S(1)}, f32[8,1,384]{2,0,1:T(8,128)S(1)}, u32[]{:S(2)}, u32[]{:S(2)}) collective-permute-start(f32[8,1,384]{2,0,1:T(8,128)S(1)} %copy.165), channel_id=1, source_target_pairs={{0,4},{4,8},{8,12},{12,16},{16,20},{20,24},{24,28},{28,0},{1,5},{5... | collective-permute-start | bytes 36872 | tf_op jit(solution)/shard_map/ppermute | solution.py:16
  203.6 10.5 %collective-permute-start.14 = (f32[8,70,1]{1,0,2:T(8,128)S(1)}, f32[8,70,1]{1,0,2:T(8,128)S(1)}, u32[]{:S(2)}, u32[]{:S(2)}) collective-permute-start(f32[8,70,1]{1,0,2:T(8,128)S(1)} %get-tuple-element.63), channel_id=1, source_target_pairs={{0,1},{1,2},{2,3},{4,5},{5,6},{6,7},{8,9},{9,10},{10,11},{12,13},{... | collective-permute-start | bytes 6728 | tf_op jit(solution)/shard_map/ppermute | solution.py:16
  212.0 4.9 %collective-permute-start.15 = (f32[8,70,1]{1,0,2:T(8,128)S(1)}, f32[8,70,1]{1,0,2:T(8,128)S(1)}, u32[]{:S(2)}, u32[]{:S(2)}) collective-permute-start(f32[8,70,1]{1,0,2:T(8,128)S(1)} %get-tuple-element.64), channel_id=1, source_target_pairs={{1,0},{2,1},{3,2},{5,4},{6,5},{7,6},{9,8},{10,9},{11,10},{13,12},{... | collective-permute-start | bytes 6728 | tf_op jit(solution)/shard_map/ppermute | solution.py:19
  220.4 2.8 %copy-start.4 = (f32[4,68,384]{2,1,0:T(8,128)S(1)}, f32[4,68,384]{2,1,0:T(8,128)}, u32[]{:S(2)}) copy-start(f32[4,68,384]{2,1,0:T(8,128)} %copy-done.1) | copy-start | bytes 1253380
  220.4 2.8 %copy-start.8 = (f32[4,68,384]{2,1,0:T(8,128)S(1)}, f32[4,68,384]{2,1,0:T(8,128)}, u32[]{:S(2)}) copy-start(f32[4,68,384]{2,1,0:T(8,128)} %copy-done.5) | copy-start | bytes 1253380
  220.4 2.8 %copy-start.12 = (f32[4,68,384]{2,1,0:T(8,128)S(1)}, f32[4,68,384]{2,1,0:T(8,128)}, u32[]{:S(2)}) copy-start(f32[4,68,384]{2,1,0:T(8,128)} %copy-done.9) | copy-start | bytes 1253380
  220.4 2.8 %copy-start.16 = (f32[4,68,384]{2,1,0:T(8,128)S(1)}, f32[4,68,384]{2,1,0:T(8,128)}, u32[]{:S(2)}) copy-start(f32[4,68,384]{2,1,0:T(8,128)} %copy-done.13) | copy-start | bytes 1253380
  (8 other events, 9.6 us)
where the time goes:
time: 227 us; the launch traced here: 226 us
  blocking collectives  99.3 us (44%)
  starting transfers between devices  58.5 us (26%)
  local copies, waits for them, and re-layouts  29.4 us (13%)
  other arithmetic  25.4 us (11%)
  waiting for transfers between devices  12.4 us (5%)
    all_gather x4, blocking collectives, local(): every_top = lax.all_gather(top_rows, 'lon', axis=1, tiled=True)  99.3 us
    ppermute x8, starting transfers between devices, extended_2(): lax.ppermute(lax.slice_in_dim(block, block.shape[dim] - width, None, axis...  34.8 us
    ppermute x8, starting transfers between devices, extended_2(): lax.ppermute(lax.slice_in_dim(block, 0, width, axis=dim), axis, backward)  23.7 us
    concatenate x4, other arithmetic, extended_2(): block = jnp.concatenate([low, block, high], axis=dim)  12.1 us
    scatter-add x4, local copies, waits for them, and re-layouts, local(): padded = padded.at[:, :, lat_cells + 1].add(at_top * folded)  9.92 us
    ppermute x8, waiting for transfers between devices, extended_2(): lax.ppermute(lax.slice_in_dim(block, 0, width, axis=dim), axis, backward)  8.54 us
    ppermute x4, local copies, waits for them, and re-layouts, extended_2(): lax.ppermute(lax.slice_in_dim(block, 0, width, axis=dim), axis, backward)  5.23 us
  transfers between devices with their start and end apart: 16, of which 4 were waited for; matrix products, arithmetic and copies ran while one was open for 6% of the time, Pallas kernels for 0%

commit v1 on v0

--- a/solution.py
+++ b/solution.py
@@ -4,6 +4,17 @@
 from jax.sharding import PartitionSpec as P
 
 PASSES = 4
+
+
+def turned_line(value, mesh_axis, dim):
+    peers = lax.axis_size(mesh_axis)
+    right = [(i, (i + 1) % peers) for i in range(peers)]
+    parts = [value]
+    for far in range(1, peers):
+        parts = [lax.ppermute(parts[0], mesh_axis, right), *parts]
+    result = jnp.concatenate(parts, axis=dim)
+    offset = (lax.axis_index(mesh_axis) + 1) * parts[-1].shape[dim]
+    return jnp.roll(result, offset, axis=dim)
 
 
 def extended_2(block, sides, width, periodic):
@@ -80,7 +91,7 @@
     for repeat in range(PASSES):
         extended = extended_2(current, (("lon", 1),), 1, True)
         top_rows = extended[:, margin : margin + lon_cells, lat_cells - 1]
-        every_top = lax.all_gather(top_rows, "lon", axis=1, tiled=True)
+        every_top = turned_line(top_rows, "lon", 1)
         folded = jnp.take(every_top, own_partners, axis=1)
         folded = jnp.concatenate(
             [jnp.zeros_like(folded[:, :1]), folded, jnp.zeros_like(folded[:, :1])], axis=1

time: 227 us -> 224 us (0.987)
  blocking collectives: 99.3 us -> 0 us
  waiting for transfers between devices: 12.4 us -> 104 us
  starting transfers between devices: 58.5 us -> 68.1 us
  other arithmetic: 25.4 us -> 20.7 us
    all_gather x4 -> x0, blocking collectives: 99.3 us -> none  [local(): every_top = lax.all_gather(top_rows, 'lon', axis=1, tiled=True)]
    ppermute x0 -> x28, waiting for transfers between devices: none -> 90.5 us  [turned_line(): parts = [lax.ppermute(parts[0], mesh_axis, right), *parts]]
    ppermute x8, starting transfers between devices: 23.7 us -> 29.2 us  [extended_2(): lax.ppermute(lax.slice_in_dim(block, 0, width, axis=dim), axis, backward)]
    concatenate x4, other arithmetic: 12.1 us -> 6.77 us  [extended_2(): block = jnp.concatenate([low, block, high], axis=dim)]
    ppermute x0 -> x28, starting transfers between devices: none -> 2.53 us  [turned_line(): parts = [lax.ppermute(parts[0], mesh_axis, right), *parts]]
  transfers between devices with their start and end apart: 16 -> 44, of which waited for: 4 -> 27; matrix products, arithmetic and copies ran while one was open for 6% -> 10% of each run, Pallas kernels for 0% -> 0%
where the time goes in v1:
time: 224 us; the launch traced here: 223 us
  waiting for transfers between devices  104 us (46%)
  starting transfers between devices  68.1 us (30%)
  local copies, waits for them, and re-layouts  29.3 us (13%)
  other arithmetic  20.7 us (9%)
    ppermute x28, waiting for transfers between devices, turned_line(): parts = [lax.ppermute(parts[0], mesh_axis, right), *parts]  90.5 us
    ppermute x8, starting transfers between devices, extended_2(): lax.ppermute(lax.slice_in_dim(block, block.shape[dim] - width, None, axis...  36.3 us
    ppermute x8, starting transfers between devices, extended_2(): lax.ppermute(lax.slice_in_dim(block, 0, width, axis=dim), axis, backward)  29.2 us
    scatter-add x4, local copies, waits for them, and re-layouts, local(): padded = padded.at[:, :, lat_cells + 1].add(at_top * folded)  9.92 us
    ppermute x8, waiting for transfers between devices, extended_2(): lax.ppermute(lax.slice_in_dim(block, 0, width, axis=dim), axis, backward)  8.99 us
    concatenate x4, other arithmetic, extended_2(): block = jnp.concatenate([low, block, high], axis=dim)  6.77 us
    ppermute x4, local copies, waits for them, and re-layouts, extended_2(): lax.ppermute(lax.slice_in_dim(block, 0, width, axis=dim), axis, backward)  5.19 us
  transfers between devices with their start and end apart: 44, of which 27 were waited for; matrix products, arithmetic and copies ran while one was open for 10% of the time, Pallas kernels for 0%

profile of v1, /device:TPU:1, one launch (start us, length us, event | category | flops | bytes accessed | tf_op | source)
XLA Modules:
  0.0 223.3 jit_solution(1231210806769968199)
XLA Ops:
  6.9 2.9 %collective-permute-start.1 = (f32[10,1,384]{2,1,0:T(1,128)S(1)}, f32[10,1,384]{2,1,0:T(1,128)S(1)}, u32[]{:S(2)}, u32[]{:S(2)}) collective-permute-start(f32[10,1,384]{2,1,0:T(1,128)S(1)} %get-tuple-element.77), channel_id=1, source_target_pairs={{4,0},{8,4},{12,8},{16,12},{20,16},{24,20},{28,24},{0,28},{5,1},{9... | collective-permute-start | bytes 46088 | tf_op jit(solution)/shard_map/ppermute | solution.py:30
  9.8 5.2 %collective-permute-done.5 = f32[10,68]{1,0:T(8,128)S(1)} collective-permute-done((f32[10,68]{1,0:T(8,128)S(1)}, f32[10,68]{1,0:T(8,128)S(1)}, u32[]{:S(2)}, u32[]{:S(2)}) %collective-permute-start.5) | collective-permute-done | bytes 2752 | tf_op jit(solution)/shard_map/ppermute | solution.py:14
  16.0 4.2 %collective-permute-done.6 = f32[10,68]{1,0:T(8,128)S(1)} collective-permute-done((f32[10,68]{1,0:T(8,128)S(1)}, f32[10,68]{1,0:T(8,128)S(1)}, u32[]{:S(2)}, u32[]{:S(2)}) %collective-permute-start.6) | collective-permute-done | bytes 2752 | tf_op jit(solution)/shard_map/ppermute | solution.py:14
  20.2 5.2 %collective-permute-done.7 = f32[10,68]{1,0:T(8,128)S(1)} collective-permute-done((f32[10,68]{1,0:T(8,128)S(1)}, f32[10,68]{1,0:T(8,128)S(1)}, u32[]{:S(2)}, u32[]{:S(2)}) %collective-permute-start.7) | collective-permute-done | bytes 2752 | tf_op jit(solution)/shard_map/ppermute | solution.py:14
  25.4 5.2 %collective-permute-done.8 = f32[10,68]{1,0:T(8,128)S(1)} collective-permute-done((f32[10,68]{1,0:T(8,128)S(1)}, f32[10,68]{1,0:T(8,128)S(1)}, u32[]{:S(2)}, u32[]{:S(2)}) %collective-permute-start.8) | collective-permute-done | bytes 2752 | tf_op jit(solution)/shard_map/ppermute | solution.py:14
  30.9 8.0 %collective-permute-start.3 = (f32[10,70,1]{1,2,0:T(1,128)S(1)}, f32[10,70,1]{1,2,0:T(1,128)S(1)}, u32[]{:S(2)}, u32[]{:S(2)}) collective-permute-start(f32[10,70,1]{1,2,0:T(1,128)S(1)} %copy.214), channel_id=1, source_target_pairs={{1,0},{2,1},{3,2},{5,4},{6,5},{7,6},{9,8},{10,9},{11,10},{13,12},{... | collective-permute-start | bytes 8408 | tf_op jit(solution)/shard_map/ppermute | solution.py:30
  39.0 3.1 %collective-permute-start.2 = (f32[10,70,1]{2,1,0:T(8,128)S(1)}, f32[10,70,1]{2,1,0:T(8,128)S(1)}, u32[]{:S(2)}, u32[]{:S(2)}) collective-permute-start(f32[10,70,1]{2,1,0:T(8,128)S(1)} %get-tuple-element.74), channel_id=1, source_target_pairs={{0,1},{1,2},{2,3},{4,5},{5,6},{6,7},{8,9},{9,10},{10,11},{12,13},{... | collective-permute-start | bytes 8408 | tf_op jit(solution)/shard_map/ppermute | solution.py:27
  42.4 4.1 %collective-permute-done.2 = f32[10,70,1]{2,1,0:T(8,128)S(1)} collective-permute-done((f32[10,70,1]{2,1,0:T(8,128)S(1)}, f32[10,70,1]{2,1,0:T(8,128)S(1)}, u32[]{:S(2)}, u32[]{:S(2)}) %collective-permute-start.2) | collective-permute-done | bytes 2832 | tf_op jit(solution)/shard_map/ppermute | solution.py:27
  49.1 3.6 %scatter-add.14 = f32[10,70,386]{2,1,0:T(8,128)S(1)} dynamic-update-slice(f32[10,70,386]{2,1,0:T(8,128)S(1)} %pad_maximum_fusion.3, f32[10,70,1]{2,1,0:T(8,128)S(1)} %copy.188, s32[]{:T(128)} %constant.157.clone.1, s32[]{:T(128)} %constant.157.clone.1, s32[]{:T(128)} %constant.163.clone.1) | dynamic-update-slice | bytes 5604 | tf_op jit(solution)/shard_map/scatter-add | solution.py:100
  55.6 5.1 %collective-permute-done.15 = f32[8,68]{1,0:T(8,128)S(1)} collective-permute-done((f32[8,68]{1,0:T(8,128)S(1)}, f32[8,68]{1,0:T(8,128)S(1)}, u32[]{:S(2)}, u32[]{:S(2)}) %collective-permute-start.15) | collective-permute-done | bytes 2208 | tf_op jit(solution)/shard_map/ppermute | solution.py:14
  60.8 5.2 %collective-permute-done.16 = f32[8,68]{1,0:T(8,128)S(1)} collective-permute-done((f32[8,68]{1,0:T(8,128)S(1)}, f32[8,68]{1,0:T(8,128)S(1)}, u32[]{:S(2)}, u32[]{:S(2)}) %collective-permute-start.16) | collective-permute-done | bytes 2208 | tf_op jit(solution)/shard_map/ppermute | solution.py:14
  65.9 5.2 %collective-permute-done.17 = f32[8,68]{1,0:T(8,128)S(1)} collective-permute-done((f32[8,68]{1,0:T(8,128)S(1)}, f32[8,68]{1,0:T(8,128)S(1)}, u32[]{:S(2)}, u32[]{:S(2)}) %collective-permute-start.17) | collective-permute-done | bytes 2208 | tf_op jit(solution)/shard_map/ppermute | solution.py:14
  71.2 4.2 %collective-permute-start.12 = (f32[8,1,384]{2,0,1:T(8,128)S(1)}, f32[8,1,384]{2,0,1:T(8,128)S(1)}, u32[]{:S(2)}, u32[]{:S(2)}) collective-permute-start(f32[8,1,384]{2,0,1:T(8,128)S(1)} %copy.190), channel_id=1, source_target_pairs={{4,0},{8,4},{12,8},{16,12},{20,16},{24,20},{28,24},{0,28},{5,1},{9... | collective-permute-start | bytes 36872 | tf_op jit(solution)/shard_map/ppermute | solution.py:30
  76.9 4.5 %collective-permute-done.19 = f32[8,68]{1,0:T(8,128)S(1)} collective-permute-done((f32[8,68]{1,0:T(8,128)S(1)}, f32[8,68]{1,0:T(8,128)S(1)}, u32[]{:S(2)}, u32[]{:S(2)}) %collective-permute-start.19) | collective-permute-done | bytes 2208 | tf_op jit(solution)/shard_map/ppermute | solution.py:14
  84.6 10.5 %collective-permute-start.13 = (f32[8,70,1]{1,0,2:T(8,128)S(1)}, f32[8,70,1]{1,0,2:T(8,128)S(1)}, u32[]{:S(2)}, u32[]{:S(2)}) collective-permute-start(f32[8,70,1]{1,0,2:T(8,128)S(1)} %get-tuple-element.70), channel_id=1, source_target_pairs={{0,1},{1,2},{2,3},{4,5},{5,6},{6,7},{8,9},{9,10},{10,11},{12,13},{... | collective-permute-start | bytes 6728 | tf_op jit(solution)/shard_map/ppermute | solution.py:27
  97.2 3.2 %collective-permute-done.14 = f32[8,70,1]{1,0,2:T(8,128)S(1)} collective-permute-done((f32[8,70,1]{1,0,2:T(8,128)S(1)}, f32[8,70,1]{1,0,2:T(8,128)S(1)}, u32[]{:S(2)}, u32[]{:S(2)}) %collective-permute-start.14) | collective-permute-done | bytes 2272 | tf_op jit(solution)/shard_map/ppermute | solution.py:30
  107.6 4.2 %collective-permute-start.23 = (f32[8,1,384]{2,0,1:T(8,128)S(1)}, f32[8,1,384]{2,0,1:T(8,128)S(1)}, u32[]{:S(2)}, u32[]{:S(2)}) collective-permute-start(f32[8,1,384]{2,0,1:T(8,128)S(1)} %copy.198), channel_id=1, source_target_pairs={{4,0},{8,4},{12,8},{16,12},{20,16},{24,20},{28,24},{0,28},{5,1},{9... | collective-permute-start | bytes 36872 | tf_op jit(solution)/shard_map/ppermute | solution.py:30
  112.2 5.3 %collective-permute-done.26 = f32[8,68]{1,0:T(8,128)S(1)} collective-permute-done((f32[8,68]{1,0:T(8,128)S(1)}, f32[8,68]{1,0:T(8,128)S(1)}, u32[]{:S(2)}, u32[]{:S(2)}) %collective-permute-start.26) | collective-permute-done | bytes 2208 | tf_op jit(solution)/shard_map/ppermute | solution.py:14
  117.5 5.2 %collective-permute-done.27 = f32[8,68]{1,0:T(8,128)S(1)} collective-permute-done((f32[8,68]{1,0:T(8,128)S(1)}, f32[8,68]{1,0:T(8,128)S(1)}, u32[]{:S(2)}, u32[]{:S(2)}) %collective-permute-start.27) | collective-permute-done | bytes 2208 | tf_op jit(solution)/shard_map/ppermute | solution.py:14
  122.7 5.2 %collective-permute-done.28 = f32[8,68]{1,0:T(8,128)S(1)} collective-permute-done((f32[8,68]{1,0:T(8,128)S(1)}, f32[8,68]{1,0:T(8,128)S(1)}, u32[]{:S(2)}, u32[]{:S(2)}) %collective-permute-start.28) | collective-permute-done | bytes 2208 | tf_op jit(solution)/shard_map/ppermute | solution.py:14
  127.8 5.2 %collective-permute-done.29 = f32[8,68]{1,0:T(8,128)S(1)} collective-permute-done((f32[8,68]{1,0:T(8,128)S(1)}, f32[8,68]{1,0:T(8,128)S(1)}, u32[]{:S(2)}, u32[]{:S(2)}) %collective-permute-start.29) | collective-permute-done | bytes 2208 | tf_op jit(solution)/shard_map/ppermute | solution.py:14
  134.8 3.4 %collective-permute-done.30 = f32[8,68]{1,0:T(8,128)S(1)} collective-permute-done((f32[8,68]{1,0:T(8,128)S(1)}, f32[8,68]{1,0:T(8,128)S(1)}, u32[]{:S(2)}, u32[]{:S(2)}) %collective-permute-start.30) | collective-permute-done | bytes 2208 | tf_op jit(solution)/shard_map/ppermute | solution.py:14
  141.3 10.6 %collective-permute-start.24 = (f32[8,70,1]{1,0,2:T(8,128)S(1)}, f32[8,70,1]{1,0,2:T(8,128)S(1)}, u32[]{:S(2)}, u32[]{:S(2)}) collective-permute-start(f32[8,70,1]{1,0,2:T(8,128)S(1)} %get-tuple-element.68), channel_id=1, source_target_pairs={{0,1},{1,2},{2,3},{4,5},{5,6},{6,7},{8,9},{9,10},{10,11},{12,13},{... | collective-permute-start | bytes 6728 | tf_op jit(solution)/shard_map/ppermute | solution.py:27
  153.9 2.9 %collective-permute-done.25 = f32[8,70,1]{1,0,2:T(8,128)S(1)} collective-permute-done((f32[8,70,1]{1,0,2:T(8,128)S(1)}, f32[8,70,1]{1,0,2:T(8,128)S(1)}, u32[]{:S(2)}, u32[]{:S(2)}) %collective-permute-start.25) | collective-permute-done | bytes 2272 | tf_op jit(solution)/shard_map/ppermute | solution.py:30
  164.4 4.1 %collective-permute-start.34 = (f32[8,1,384]{2,0,1:T(8,128)S(1)}, f32[8,1,384]{2,0,1:T(8,128)S(1)}, u32[]{:S(2)}, u32[]{:S(2)}) collective-permute-start(f32[8,1,384]{2,0,1:T(8,128)S(1)} %copy.206), channel_id=1, source_target_pairs={{4,0},{8,4},{12,8},{16,12},{20,16},{24,20},{28,24},{0,28},{5,1},{9... | collective-permute-start | bytes 36872 | tf_op jit(solution)/shard_map/ppermute | solution.py:30
  168.9 5.1 %collective-permute-done.37 = f32[8,68]{1,0:T(8,128)S(1)} collective-permute-done((f32[8,68]{1,0:T(8,128)S(1)}, f32[8,68]{1,0:T(8,128)S(1)}, u32[]{:S(2)}, u32[]{:S(2)}) %collective-permute-start.37) | collective-permute-done | bytes 2208 | tf_op jit(solution)/shard_map/ppermute | solution.py:14
  174.1 5.4 %collective-permute-done.38 = f32[8,68]{1,0:T(8,128)S(1)} collective-permute-done((f32[8,68]{1,0:T(8,128)S(1)}, f32[8,68]{1,0:T(8,128)S(1)}, u32[]{:S(2)}, u32[]{:S(2)}) %collective-permute-start.38) | collective-permute-done | bytes 2208 | tf_op jit(solution)/shard_map/ppermute | solution.py:14
  179.4 5.2 %collective-permute-done.39 = f32[8,68]{1,0:T(8,128)S(1)} collective-permute-done((f32[8,68]{1,0:T(8,128)S(1)}, f32[8,68]{1,0:T(8,128)S(1)}, u32[]{:S(2)}, u32[]{:S(2)}) %collective-permute-start.39) | collective-permute-done | bytes 2208 | tf_op jit(solution)/shard_map/ppermute | solution.py:14
  184.6 5.2 %collective-permute-done.40 = f32[8,68]{1,0:T(8,128)S(1)} collective-permute-done((f32[8,68]{1,0:T(8,128)S(1)}, f32[8,68]{1,0:T(8,128)S(1)}, u32[]{:S(2)}, u32[]{:S(2)}) %collective-permute-start.40) | collective-permute-done | bytes 2208 | tf_op jit(solution)/shard_map/ppermute | solution.py:14
  191.5 3.4 %collective-permute-done.41 = f32[8,68]{1,0:T(8,128)S(1)} collective-permute-done((f32[8,68]{1,0:T(8,128)S(1)}, f32[8,68]{1,0:T(8,128)S(1)}, u32[]{:S(2)}, u32[]{:S(2)}) %collective-permute-start.41) | collective-permute-done | bytes 2208 | tf_op jit(solution)/shard_map/ppermute | solution.py:14
  198.1 10.6 %collective-permute-start.35 = (f32[8,70,1]{1,0,2:T(8,128)S(1)}, f32[8,70,1]{1,0,2:T(8,128)S(1)}, u32[]{:S(2)}, u32[]{:S(2)}) collective-permute-start(f32[8,70,1]{1,0,2:T(8,128)S(1)} %get-tuple-element.66), channel_id=1, source_target_pairs={{0,1},{1,2},{2,3},{4,5},{5,6},{6,7},{8,9},{9,10},{10,11},{12,13},{... | collective-permute-start | bytes 6728 | tf_op jit(solution)/shard_map/ppermute | solution.py:27
  210.7 2.9 %collective-permute-done.36 = f32[8,70,1]{1,0,2:T(8,128)S(1)} collective-permute-done((f32[8,70,1]{1,0,2:T(8,128)S(1)}, f32[8,70,1]{1,0,2:T(8,128)S(1)}, u32[]{:S(2)}, u32[]{:S(2)}) %collective-permute-start.36) | collective-permute-done | bytes 2272 | tf_op jit(solution)/shard_map/ppermute | solution.py:30
  (210 shorter events, 58.6 us)
Async XLA Ops:
  3.5 6.3 %collective-permute-start.4 = (f32[10,68]{1,0:T(8,128)S(1)}, f32[10,68]{1,0:T(8,128)S(1)}, u32[]{:S(2)}, u32[]{:S(2)}) collective-permute-start(f32[10,68]{1,0:T(8,128)S(1)} %bitcast.89), channel_id=1, source_target_pairs={{0,4},{4,8},{8,12},{12,16},{16,20},{20,24},{24,28},{28,0},{1,5},{5... | collective-permute-start | bytes 8168 | tf_op jit(solution)/shard_map/ppermute | solution.py:14
  5.6 25.0 %collective-permute-start = (f32[10,1,384]{2,1,0:T(1,128)S(1)}, f32[10,1,384]{2,1,0:T(1,128)S(1)}, u32[]{:S(2)}, u32[]{:S(2)}) collective-permute-start(f32[10,1,384]{2,1,0:T(1,128)S(1)} %get-tuple-element.76), channel_id=1, source_target_pairs={{0,4},{4,8},{8,12},{12,16},{16,20},{20,24},{24,28},{28,0},{1,5},{5... | collective-permute-start | bytes 46088 | tf_op jit(solution)/shard_map/ppermute | solution.py:27
  6.9 23.7 %collective-permute-start.1 = (f32[10,1,384]{2,1,0:T(1,128)S(1)}, f32[10,1,384]{2,1,0:T(1,128)S(1)}, u32[]{:S(2)}, u32[]{:S(2)}) collective-permute-start(f32[10,1,384]{2,1,0:T(1,128)S(1)} %get-tuple-element.77), channel_id=1, source_target_pairs={{4,0},{8,4},{12,8},{16,12},{20,16},{24,20},{28,24},{0,28},{5,1},{9... | collective-permute-start | bytes 46088 | tf_op jit(solution)/shard_map/ppermute | solution.py:30
  9.8 5.2 %collective-permute-start.5 = (f32[10,68]{1,0:T(8,128)S(1)}, f32[10,68]{1,0:T(8,128)S(1)}, u32[]{:S(2)}, u32[]{:S(2)}) collective-permute-start(f32[10,68]{1,0:T(8,128)S(1)} %collective-permute-done.4), channel_id=1, source_target_pairs={{0,4},{4,8},{8,12},{12,16},{16,20},{20,24},{24,28},{28,0},{1,5},{5... | collective-permute-start | bytes 8168 | tf_op jit(solution)/shard_map/ppermute | solution.py:14
  15.0 5.2 %collective-permute-start.6 = (f32[10,68]{1,0:T(8,128)S(1)}, f32[10,68]{1,0:T(8,128)S(1)}, u32[]{:S(2)}, u32[]{:S(2)}) collective-permute-start(f32[10,68]{1,0:T(8,128)S(1)} %collective-permute-done.5), channel_id=1, source_target_pairs={{0,4},{4,8},{8,12},{12,16},{16,20},{20,24},{24,28},{28,0},{1,5},{5... | collective-permute-start | bytes 8168 | tf_op jit(solution)/shard_map/ppermute | solution.py:14
  20.2 5.2 %collective-permute-start.7 = (f32[10,68]{1,0:T(8,128)S(1)}, f32[10,68]{1,0:T(8,128)S(1)}, u32[]{:S(2)}, u32[]{:S(2)}) collective-permute-start(f32[10,68]{1,0:T(8,128)S(1)} %collective-permute-done.6), channel_id=1, source_target_pairs={{0,4},{4,8},{8,12},{12,16},{16,20},{20,24},{24,28},{28,0},{1,5},{5... | collective-permute-start | bytes 8168 | tf_op jit(solution)/shard_map/ppermute | solution.py:14
  25.4 5.2 %collective-permute-start.8 = (f32[10,68]{1,0:T(8,128)S(1)}, f32[10,68]{1,0:T(8,128)S(1)}, u32[]{:S(2)}, u32[]{:S(2)}) collective-permute-start(f32[10,68]{1,0:T(8,128)S(1)} %collective-permute-done.7), channel_id=1, source_target_pairs={{0,4},{4,8},{8,12},{12,16},{16,20},{20,24},{24,28},{28,0},{1,5},{5... | collective-permute-start | bytes 8168 | tf_op jit(solution)/shard_map/ppermute | solution.py:14
  30.6 11.6 %collective-permute-start.9 = (f32[10,68]{1,0:T(8,128)S(1)}, f32[10,68]{1,0:T(8,128)S(1)}, u32[]{:S(2)}, u32[]{:S(2)}) collective-permute-start(f32[10,68]{1,0:T(8,128)S(1)} %collective-permute-done.8), channel_id=1, source_target_pairs={{0,4},{4,8},{8,12},{12,16},{16,20},{20,24},{24,28},{28,0},{1,5},{5... | collective-permute-start | bytes 8168 | tf_op jit(solution)/shard_map/ppermute | solution.py:14
  30.9 11.3 %collective-permute-start.3 = (f32[10,70,1]{1,2,0:T(1,128)S(1)}, f32[10,70,1]{1,2,0:T(1,128)S(1)}, u32[]{:S(2)}, u32[]{:S(2)}) collective-permute-start(f32[10,70,1]{1,2,0:T(1,128)S(1)} %copy.214), channel_id=1, source_target_pairs={{1,0},{2,1},{3,2},{5,4},{6,5},{7,6},{9,8},{10,9},{11,10},{13,12},{... | collective-permute-start | bytes 8408 | tf_op jit(solution)/shard_map/ppermute | solution.py:30
  39.0 7.5 %collective-permute-start.2 = (f32[10,70,1]{2,1,0:T(8,128)S(1)}, f32[10,70,1]{2,1,0:T(8,128)S(1)}, u32[]{:S(2)}, u32[]{:S(2)}) collective-permute-start(f32[10,70,1]{2,1,0:T(8,128)S(1)} %get-tuple-element.74), channel_id=1, source_target_pairs={{0,1},{1,2},{2,3},{4,5},{5,6},{6,7},{8,9},{9,10},{10,11},{12,13},{... | collective-permute-start | bytes 8408 | tf_op jit(solution)/shard_map/ppermute | solution.py:27
  42.1 5.5 %collective-permute-start.10 = (f32[10,68]{1,0:T(8,128)S(1)}, f32[10,68]{1,0:T(8,128)S(1)}, u32[]{:S(2)}, u32[]{:S(2)}) collective-permute-start(f32[10,68]{1,0:T(8,128)S(1)} %collective-permute-done.9), channel_id=1, source_target_pairs={{0,4},{4,8},{8,12},{12,16},{16,20},{20,24},{24,28},{28,0},{1,5},{5... | collective-permute-start | bytes 8168 | tf_op jit(solution)/shard_map/ppermute | solution.py:14
  55.6 5.2 %collective-permute-start.15 = (f32[8,68]{1,0:T(8,128)S(1)}, f32[8,68]{1,0:T(8,128)S(1)}, u32[]{:S(2)}, u32[]{:S(2)}) collective-permute-start(f32[8,68]{1,0:T(8,128)S(1)} %slice_reduce_fusion.2), channel_id=1, source_target_pairs={{0,4},{4,8},{8,12},{12,16},{16,20},{20,24},{24,28},{28,0},{1,5},{5... | collective-permute-start | bytes 6536 | tf_op jit(solution)/shard_map/ppermute | solution.py:14
  71.1 10.3 %collective-permute-start.11 = (f32[8,1,384]{2,0,1:T(8,128)S(1)}, f32[8,1,384]{2,0,1:T(8,128)S(1)}, u32[]{:S(2)}, u32[]{:S(2)}) collective-permute-start(f32[8,1,384]{2,0,1:T(8,128)S(1)} %copy.189), channel_id=1, source_target_pairs={{0,4},{4,8},{8,12},{12,16},{16,20},{20,24},{24,28},{28,0},{1,5},{5... | collective-permute-start | bytes 36872 | tf_op jit(solution)/shard_map/ppermute | solution.py:27
  71.2 10.8 %collective-permute-start.12 = (f32[8,1,384]{2,0,1:T(8,128)S(1)}, f32[8,1,384]{2,0,1:T(8,128)S(1)}, u32[]{:S(2)}, u32[]{:S(2)}) collective-permute-start(f32[8,1,384]{2,0,1:T(8,128)S(1)} %copy.190), channel_id=1, source_target_pairs={{4,0},{8,4},{12,8},{16,12},{20,16},{24,20},{28,24},{0,28},{5,1},{9... | collective-permute-start | bytes 36872 | tf_op jit(solution)/shard_map/ppermute | solution.py:30
  76.2 5.2 %collective-permute-start.19 = (f32[8,68]{1,0:T(8,128)S(1)}, f32[8,68]{1,0:T(8,128)S(1)}, u32[]{:S(2)}, u32[]{:S(2)}) collective-permute-start(f32[8,68]{1,0:T(8,128)S(1)} %collective-permute-done.18), channel_id=1, source_target_pairs={{0,4},{4,8},{8,12},{12,16},{16,20},{20,24},{24,28},{28,0},{1,5},{5... | collective-permute-start | bytes 6536 | tf_op jit(solution)/shard_map/ppermute | solution.py:14
  81.4 15.7 %collective-permute-start.20 = (f32[8,68]{1,0:T(8,128)S(1)}, f32[8,68]{1,0:T(8,128)S(1)}, u32[]{:S(2)}, u32[]{:S(2)}) collective-permute-start(f32[8,68]{1,0:T(8,128)S(1)} %collective-permute-done.19), channel_id=1, source_target_pairs={{0,4},{4,8},{8,12},{12,16},{16,20},{20,24},{24,28},{28,0},{1,5},{5... | collective-permute-start | bytes 6536 | tf_op jit(solution)/shard_map/ppermute | solution.py:14
  84.6 12.6 %collective-permute-start.13 = (f32[8,70,1]{1,0,2:T(8,128)S(1)}, f32[8,70,1]{1,0,2:T(8,128)S(1)}, u32[]{:S(2)}, u32[]{:S(2)}) collective-permute-start(f32[8,70,1]{1,0,2:T(8,128)S(1)} %get-tuple-element.70), channel_id=1, source_target_pairs={{0,1},{1,2},{2,3},{4,5},{5,6},{6,7},{8,9},{9,10},{10,11},{12,13},{... | collective-permute-start | bytes 6728 | tf_op jit(solution)/shard_map/ppermute | solution.py:27
  95.1 5.2 %collective-permute-start.14 = (f32[8,70,1]{1,0,2:T(8,128)S(1)}, f32[8,70,1]{1,0,2:T(8,128)S(1)}, u32[]{:S(2)}, u32[]{:S(2)}) collective-permute-start(f32[8,70,1]{1,0,2:T(8,128)S(1)} %get-tuple-element.71), channel_id=1, source_target_pairs={{1,0},{2,1},{3,2},{5,4},{6,5},{7,6},{9,8},{10,9},{11,10},{13,12},{... | collective-permute-start | bytes 6728 | tf_op jit(solution)/shard_map/ppermute | solution.py:30
  97.1 5.5 %collective-permute-start.21 = (f32[8,68]{1,0:T(8,128)S(1)}, f32[8,68]{1,0:T(8,128)S(1)}, u32[]{:S(2)}, u32[]{:S(2)}) collective-permute-start(f32[8,68]{1,0:T(8,128)S(1)} %collective-permute-done.20), channel_id=1, source_target_pairs={{0,4},{4,8},{8,12},{12,16},{16,20},{20,24},{24,28},{28,0},{1,5},{5... | collective-permute-start | bytes 6536 | tf_op jit(solution)/shard_map/ppermute | solution.py:14
  107.5 30.6 %collective-permute-start.22 = (f32[8,1,384]{2,0,1:T(8,128)S(1)}, f32[8,1,384]{2,0,1:T(8,128)S(1)}, u32[]{:S(2)}, u32[]{:S(2)}) collective-permute-start(f32[8,1,384]{2,0,1:T(8,128)S(1)} %copy.197), channel_id=1, source_target_pairs={{0,4},{4,8},{8,12},{12,16},{16,20},{20,24},{24,28},{28,0},{1,5},{5... | collective-permute-start | bytes 36872 | tf_op jit(solution)/shard_map/ppermute | solution.py:27
  107.6 31.1 %collective-permute-start.23 = (f32[8,1,384]{2,0,1:T(8,128)S(1)}, f32[8,1,384]{2,0,1:T(8,128)S(1)}, u32[]{:S(2)}, u32[]{:S(2)}) collective-permute-start(f32[8,1,384]{2,0,1:T(8,128)S(1)} %copy.198), channel_id=1, source_target_pairs={{4,0},{8,4},{12,8},{16,12},{20,16},{24,20},{28,24},{0,28},{5,1},{9... | collective-permute-start | bytes 36872 | tf_op jit(solution)/shard_map/ppermute | solution.py:30
  112.1 5.4 %collective-permute-start.26 = (f32[8,68]{1,0:T(8,128)S(1)}, f32[8,68]{1,0:T(8,128)S(1)}, u32[]{:S(2)}, u32[]{:S(2)}) collective-permute-start(f32[8,68]{1,0:T(8,128)S(1)} %slice_reduce_fusion.1), channel_id=1, source_target_pairs={{0,4},{4,8},{8,12},{12,16},{16,20},{20,24},{24,28},{28,0},{1,5},{5... | collective-permute-start | bytes 6536 | tf_op jit(solution)/shard_map/ppermute | solution.py:14
  138.1 15.7 %collective-permute-start.31 = (f32[8,68]{1,0:T(8,128)S(1)}, f32[8,68]{1,0:T(8,128)S(1)}, u32[]{:S(2)}, u32[]{:S(2)}) collective-permute-start(f32[8,68]{1,0:T(8,128)S(1)} %collective-permute-done.30), channel_id=1, source_target_pairs={{0,4},{4,8},{8,12},{12,16},{16,20},{20,24},{24,28},{28,0},{1,5},{5... | collective-permute-start | bytes 6536 | tf_op jit(solution)/shard_map/ppermute | solution.py:14
  141.3 12.6 %collective-permute-start.24 = (f32[8,70,1]{1,0,2:T(8,128)S(1)}, f32[8,70,1]{1,0,2:T(8,128)S(1)}, u32[]{:S(2)}, u32[]{:S(2)}) collective-permute-start(f32[8,70,1]{1,0,2:T(8,128)S(1)} %get-tuple-element.68), channel_id=1, source_target_pairs={{0,1},{1,2},{2,3},{4,5},{5,6},{6,7},{8,9},{9,10},{10,11},{12,13},{... | collective-permute-start | bytes 6728 | tf_op jit(solution)/shard_map/ppermute | solution.py:27
  153.8 5.5 %collective-permute-start.32 = (f32[8,68]{1,0:T(8,128)S(1)}, f32[8,68]{1,0:T(8,128)S(1)}, u32[]{:S(2)}, u32[]{:S(2)}) collective-permute-start(f32[8,68]{1,0:T(8,128)S(1)} %collective-permute-done.31), channel_id=1, source_target_pairs={{0,4},{4,8},{8,12},{12,16},{16,20},{20,24},{24,28},{28,0},{1,5},{5... | collective-permute-start | bytes 6536 | tf_op jit(solution)/shard_map/ppermute | solution.py:14
  164.3 30.6 %collective-permute-start.33 = (f32[8,1,384]{2,0,1:T(8,128)S(1)}, f32[8,1,384]{2,0,1:T(8,128)S(1)}, u32[]{:S(2)}, u32[]{:S(2)}) collective-permute-start(f32[8,1,384]{2,0,1:T(8,128)S(1)} %copy.205), channel_id=1, source_target_pairs={{0,4},{4,8},{8,12},{12,16},{16,20},{20,24},{24,28},{28,0},{1,5},{5... | collective-permute-start | bytes 36872 | tf_op jit(solution)/shard_map/ppermute | solution.py:27
  164.4 31.1 %collective-permute-start.34 = (f32[8,1,384]{2,0,1:T(8,128)S(1)}, f32[8,1,384]{2,0,1:T(8,128)S(1)}, u32[]{:S(2)}, u32[]{:S(2)}) collective-permute-start(f32[8,1,384]{2,0,1:T(8,128)S(1)} %copy.206), channel_id=1, source_target_pairs={{4,0},{8,4},{12,8},{16,12},{20,16},{24,20},{28,24},{0,28},{5,1},{9... | collective-permute-start | bytes 36872 | tf_op jit(solution)/shard_map/ppermute | solution.py:30
  168.9 5.2 %collective-permute-start.37 = (f32[8,68]{1,0:T(8,128)S(1)}, f32[8,68]{1,0:T(8,128)S(1)}, u32[]{:S(2)}, u32[]{:S(2)}) collective-permute-start(f32[8,68]{1,0:T(8,128)S(1)} %slice_reduce_fusion), channel_id=1, source_target_pairs={{0,4},{4,8},{8,12},{12,16},{16,20},{20,24},{24,28},{28,0},{1,5},{5... | collective-permute-start | bytes 6536 | tf_op jit(solution)/shard_map/ppermute | solution.py:14
  174.1 5.4 %collective-permute-start.38 = (f32[8,68]{1,0:T(8,128)S(1)}, f32[8,68]{1,0:T(8,128)S(1)}, u32[]{:S(2)}, u32[]{:S(2)}) collective-permute-start(f32[8,68]{1,0:T(8,128)S(1)} %collective-permute-done.37), channel_id=1, source_target_pairs={{0,4},{4,8},{8,12},{12,16},{16,20},{20,24},{24,28},{28,0},{1,5},{5... | collective-permute-start | bytes 6536 | tf_op jit(solution)/shard_map/ppermute | solution.py:14
  194.9 15.7 %collective-permute-start.42 = (f32[8,68]{1,0:T(8,128)S(1)}, f32[8,68]{1,0:T(8,128)S(1)}, u32[]{:S(2)}, u32[]{:S(2)}) collective-permute-start(f32[8,68]{1,0:T(8,128)S(1)} %collective-permute-done.41), channel_id=1, source_target_pairs={{0,4},{4,8},{8,12},{12,16},{16,20},{20,24},{24,28},{28,0},{1,5},{5... | collective-permute-start | bytes 6536 | tf_op jit(solution)/shard_map/ppermute | solution.py:14
  198.1 12.7 %collective-permute-start.35 = (f32[8,70,1]{1,0,2:T(8,128)S(1)}, f32[8,70,1]{1,0,2:T(8,128)S(1)}, u32[]{:S(2)}, u32[]{:S(2)}) collective-permute-start(f32[8,70,1]{1,0,2:T(8,128)S(1)} %get-tuple-element.66), channel_id=1, source_target_pairs={{0,1},{1,2},{2,3},{4,5},{5,6},{6,7},{8,9},{9,10},{10,11},{12,13},{... | collective-permute-start | bytes 6728 | tf_op jit(solution)/shard_map/ppermute | solution.py:27
  210.7 5.5 %collective-permute-start.43 = (f32[8,68]{1,0:T(8,128)S(1)}, f32[8,68]{1,0:T(8,128)S(1)}, u32[]{:S(2)}, u32[]{:S(2)}) collective-permute-start(f32[8,68]{1,0:T(8,128)S(1)} %collective-permute-done.42), channel_id=1, source_target_pairs={{0,4},{4,8},{8,12},{12,16},{16,20},{20,24},{24,28},{28,0},{1,5},{5... | collective-permute-start | bytes 6536 | tf_op jit(solution)/shard_map/ppermute | solution.py:14
  (39 other events, 255.6 us)
